TPU v7x, 128 devices: a whole 4x4x4 slice. The times are simulated.
128 devices in a mesh: seq: 8 (over y, x_hi), hid: 16 (over z, x_lo, core).
Axes of the slice: x: 4 (x_hi: 2, x_lo: 2; x = x_hi * 2 + x_lo), y: 4, z: 4, core: 2. Of those that a mesh axis runs over, the one named last changes fastest.
Arguments:
- tokens: bfloat16 [5120, 5120], P('seq', 'hid'), may hold values from -18 to 18
- clip_id: int32 [5120], P('seq'), may hold values from 0 to 7, never falling along the last dimension, each value on 1 to 3200 neighbouring positions
- clip_step: int32 [8], replicated, may hold values from 0 to 31
- mod_table: float32 [32, 6, 5120], replicated, may hold values from -3 to 3
- w_query: bfloat16 [5120, 4096], P(None, 'hid'), may hold values from -3 to 3
- w_key: bfloat16 [5120, 4096], P(None, 'hid'), may hold values from -3 to 3
- w_value: bfloat16 [5120, 4096], P(None, 'hid'), may hold values from -0.078125 to 0.078125
- q_gain: float32 [4096], P('hid'), may hold values from 0.4 to 6
- k_gain: float32 [4096], P('hid'), may hold values from 0.4 to 6
- w_out: bfloat16 [4096, 5120], P('hid'), may hold values from -0.125 to 0.125
- w_up: bfloat16 [5120, 8192], P(None, 'hid'), may hold values from -0.078125 to 0.078125
- w_down: bfloat16 [8192, 5120], P('hid'), may hold values from -0.09375 to 0.09375
Outputs:
- block_out: bfloat16 [5120, 5120], P('seq', 'hid')
Inputs may be any that keep to these rules, and one draw needn't show every extreme that they name: `clip_id`: clip numbers never fall along the tokens; every clip 0 to 7 holds 1 to 3200 tokens, and one holds exactly 3200.
All inputs are finite; a program needn't handle non-finite values.
Results may differ from a plain program's by a relative error of at most 0.018.
Values may be sent and summed in bfloat16 or wider, within the bound.
A program may use at most 128 MiB of HBM per device.

v0:
```python
import jax
import jax.numpy as jnp
from jax import lax
from jax.sharding import PartitionSpec as P

HEAD_DIM = 128
epsilon = 1e-06
highest = lax.Precision.HIGHEST
masked_low = -1e30


def table_rows(step_hot, mod_table, component, col_start, col_count):
    table = lax.dynamic_slice_in_dim(mod_table[:, component, :], col_start, col_count, 1)
    return jnp.dot(step_hot, table, precision=highest, preferred_element_type=jnp.float32)


def modulated(values, row_mean, spread_sq, scale_rows, shift_rows):
    scaled = (values - row_mean) * lax.rsqrt(spread_sq + epsilon)
    return (scaled * (1.0 + scale_rows) + shift_rows).astype(jnp.bfloat16)


def shared_moments(values, full_width):
    summed, squares = lax.psum((jnp.sum(values, axis=1), jnp.sum(values * values, axis=1)), "hid")
    row_mean = (summed / full_width)[:, None]
    return (row_mean, (squares / full_width)[:, None] - row_mean * row_mean)


def stored(values):
    return lax.optimization_barrier(values.astype(jnp.bfloat16)).astype(jnp.float32)


def shards(
    tokens,
    clip_id,
    clip_step,
    mod_table,
    w_query,
    w_key,
    w_value,
    q_gain,
    k_gain,
    w_out,
    w_up,
    w_down,
):
    tok_rows, feat_part = tokens.shape
    full_width = mod_table.shape[2]
    col_start = lax.axis_index("hid") * feat_part
    head_cols = w_query.shape[1]
    heads_here = head_cols // HEAD_DIM
    all_cols = head_cols * lax.axis_size("hid")
    clip_hot = (
        clip_id[:, None] == jnp.arange(clip_step.shape[0], dtype=jnp.int32)[None, :]
    ).astype(jnp.float32)
    token_step = jnp.dot(
        clip_hot,
        clip_step.astype(jnp.float32),
        precision=highest,
        preferred_element_type=jnp.float32,
    )
    step_hot = (
        token_step[:, None] == jnp.arange(mod_table.shape[0], dtype=jnp.float32)[None, :]
    ).astype(jnp.float32)
    own_rows = tokens.astype(jnp.float32)
    gate_ffn = table_rows(step_hot, mod_table, 5, col_start, feat_part)
    row_mean, spread_sq = shared_moments(own_rows, full_width)
    normed = modulated(
        own_rows,
        row_mean,
        spread_sq,
        table_rows(step_hot, mod_table, 1, col_start, feat_part),
        table_rows(step_hot, mod_table, 0, col_start, feat_part),
    )
    pieces = lax.all_gather(normed, "hid", axis=1, tiled=True)

    def accumulate(weight):
        return jnp.dot(pieces, weight, preferred_element_type=jnp.float32)

    queries = accumulate(w_query)
    key_proj = accumulate(w_key)
    value_proj = accumulate(w_value)
    q_sq, k_sq = lax.psum(
        (jnp.sum(queries * queries, axis=1), jnp.sum(key_proj * key_proj, axis=1)), "hid"
    )
    q_normed = (queries * lax.rsqrt(q_sq / all_cols + epsilon)[:, None] * q_gain).astype(
        jnp.bfloat16
    )
    k_normed = (key_proj * lax.rsqrt(k_sq / all_cols + epsilon)[:, None] * k_gain).astype(
        jnp.bfloat16
    )
    value_rows = value_proj.astype(jnp.bfloat16)
    clip_marks = clip_id.astype(jnp.bfloat16)
    q_heads = q_normed.reshape(tok_rows, heads_here, HEAD_DIM)
    score_scale = HEAD_DIM ** (-0.5)

    def tile_update(running, tile):
        key_tile, value_tile, mark_tile = tile
        old_best, old_sum, old_acc = running
        scores = (
            jnp.einsum("qhd,khd->hqk", q_heads, key_tile, preferred_element_type=jnp.float32)
            * score_scale
        )
        same_clip = (clip_marks[:, None] == mark_tile[None, :])[None]
        masked = jnp.where(same_clip, scores, masked_low)
        row_best = jnp.maximum(old_best, jnp.max(masked, axis=2))
        weights = jnp.where(same_clip, jnp.exp(masked - row_best[:, :, None]), 0.0)
        rescale = jnp.exp(old_best - row_best)
        new_sum = old_sum * rescale + jnp.sum(weights, axis=2)
        mixed = jnp.einsum(
            "hqk,khd->hqd",
            weights.astype(jnp.bfloat16),
            value_tile,
            preferred_element_type=jnp.float32,
        )
        return (row_best, new_sum, old_acc * rescale[:, :, None] + mixed)

    start_state = (
        jnp.full((heads_here, tok_rows), masked_low, jnp.float32),
        jnp.zeros((heads_here, tok_rows), jnp.float32),
        jnp.zeros((heads_here, tok_rows, HEAD_DIM), jnp.float32),
    )
    key_piece = lax.all_gather(k_normed, "seq", axis=0, tiled=True)
    value_piece = lax.all_gather(value_rows, "seq", axis=0, tiled=True)
    mark_piece = lax.all_gather(clip_marks, "seq", axis=0, tiled=True)
    tile_count = key_piece.shape[0] // tok_rows
    tiles = (
        key_piece.reshape(tile_count, tok_rows, heads_here, HEAD_DIM),
        value_piece.reshape(tile_count, tok_rows, heads_here, HEAD_DIM),
        mark_piece.reshape(tile_count, tok_rows),
    )

    def tile_step(inner, tile):
        return (tile_update(inner, tile), None)

    finished, unused = lax.scan(tile_step, start_state, tiles)
    best_all, sum_all, acc_all = finished
    attended = (
        (acc_all / sum_all[:, :, None])
        .astype(jnp.bfloat16)
        .transpose(1, 0, 2)
        .reshape(tok_rows, head_cols)
    )
    out_terms = jnp.dot(attended, w_out, preferred_element_type=jnp.float32)
    attn_own = lax.psum_scatter(
        out_terms.astype(jnp.bfloat16), "hid", scatter_dimension=1, tiled=True
    ).astype(jnp.float32)
    gate_attn = table_rows(step_hot, mod_table, 2, col_start, feat_part)
    residual_own = stored(own_rows + gate_attn * attn_own)
    row_mean, spread_sq = shared_moments(residual_own, full_width)
    normed_ffn = modulated(
        residual_own,
        row_mean,
        spread_sq,
        table_rows(step_hot, mod_table, 4, col_start, feat_part),
        table_rows(step_hot, mod_table, 3, col_start, feat_part),
    )
    up_proj = jnp.dot(
        lax.all_gather(normed_ffn, "hid", axis=1, tiled=True),
        w_up,
        preferred_element_type=jnp.float32,
    )
    hidden = jax.nn.gelu(up_proj, approximate=True).astype(jnp.bfloat16)
    ffn_own = lax.psum_scatter(
        jnp.dot(hidden, w_down, preferred_element_type=jnp.float32).astype(jnp.bfloat16),
        "hid",
        scatter_dimension=1,
        tiled=True,
    ).astype(jnp.float32)
    return (residual_own + gate_ffn * ffn_own).astype(jnp.bfloat16)


def solution(mesh):
    placed = (
        P("seq", "hid"),
        P("seq"),
        P(),
        P(),
        P(None, "hid"),
        P(None, "hid"),
        P(None, "hid"),
        P("hid"),
        P("hid"),
        P("hid", None),
        P(None, "hid"),
        P("hid", None),
    )
    return jax.shard_map(
        shards, mesh=mesh, in_specs=placed, out_specs=P("seq", "hid"), check_vma=False
    )
```

profile of v0, /device:TPU:0, one launch (start us, length us, event | category | flops | bytes accessed | tf_op | source)
XLA Modules:
  0.0 604.5 jit_solution(17240052192492611231)
XLA Ops:
  7.9 4.1 fusion.72
  11.9 32.1 %all-reduce.2 = (f32[640]{0:T(1024)S(1)}, f32[640]{0:T(1024)S(1)}) all-reduce(f32[640]{0:T(1024)S(1)} %get-tuple-element.124, f32[640]{0:T(1024)S(1)} %get-tuple-element.123), channel_id=1, replica_groups=mesh['seq'=8,'hid'=16] {'hid'}, use_global_device_ids=true, to_apply=%region_3.0 | all-reduce | flops 1280 | bytes 10240 | tf_op jit(solution)/shard_map/psum | solution.py:23
  48.5 42.2 %all-gather.6.cloned.1.call-done = bf16[640,5120]{0,1:T(8,128)(2,1)} async-done(((bf16[640,320]{0,1:T(8,128)(2,1)}), bf16[640,5120]{0,1:T(8,128)(2,1)}) %all-gather.6.cloned.1.call-update) | async-done | bytes 6553616 | tf_op jit(solution)/shard_map/all_gather | solution.py:74
  90.7 6.0 multiply_reduce_fusion.1
  97.0 3.1 multiply_reduce_fusion
  100.1 30.5 %all-reduce.1 = (f32[640]{0:T(1024)S(1)}, f32[640]{0:T(1024)S(1)}) all-reduce(f32[640]{0:T(1024)S(1)} %get-tuple-element.163, f32[640]{0:T(1024)S(1)} %get-tuple-element.165), channel_id=1, replica_groups=mesh['seq'=8,'hid'=16] {'hid'}, use_global_device_ids=true, to_apply=%region_5.0 | all-reduce | flops 1280 | bytes 10240 | tf_op jit(solution)/shard_map/psum | solution.py:82
  131.6 6.3 %convolution_convert_fusion.2 = bf16[640,256]{1,0:T(8,128)(2,1)} fusion(bf16[640,5120]{0,1:T(8,128)(2,1)} %all-gather.6.cloned.1.call-done, bf16[5120,256]{1,0:T(8,128)(2,1)} %param.20), kind=kOutput, calls=%fused_computation.56 | convolution fusion | flops 1677885440 | bytes 9502720 | tf_op jit(solution)/shard_map/dot_general | solution.py:77
  138.0 34.2 %all-gather = bf16[8,1,640]{2,1,0:T(2,128)(2,1)S(1)} all-gather(bf16[1,1,640]{2,1,0:T(2,128)(2,1)S(1)} %reshape.75), channel_id=1, replica_groups=mesh['seq'=8,'hid'=16] {'seq'}, dimensions={0}, use_global_device_ids=true | all-gather | bytes 11520 | tf_op jit(solution)/shard_map/all_gather | solution.py:124
  173.6 14.6 %all-gather.8.cloned.1.call-done = bf16[5120,256]{0,1:T(8,128)(2,1)} async-done(((bf16[640,256]{0,1:T(8,128)(2,1)}), bf16[5120,256]{0,1:T(8,128)(2,1)}) %all-gather.8.cloned.1.call-update) | async-done | bytes 2621456 | tf_op jit(solution)/shard_map/all_gather | solution.py:122
  188.2 3.8 copy.35
  192.0 4.8 copy.28
  196.7 49.9 %all-gather.10.cloned.1.call-done = bf16[5120,256]{1,0:T(8,128)(2,1)} async-done(((bf16[640,256]{1,0:T(8,128)(2,1)}), bf16[5120,256]{1,0:T(8,128)(2,1)}) %all-gather.10.cloned.1.call-update) | async-done | bytes 2621456 | tf_op jit(solution)/shard_map/all_gather | solution.py:123
  246.7 4.9 reshape.73
  251.6 84.6 %while.15 = (s32[]{:T(128)}, f32[2,640]{1,0:T(2,128)S(1)}, f32[2,640]{1,0:T(2,128)S(1)}, f32[2,640,128]{2,1,0:T(8,128)}, bf16[640]{0:T(1024)(128)(2,1)S(1)}, /*i...) while((s32[]{:T(128)}, f32[2,640]{1,0:T(2,128)S(1)}, ...), condition=%wide.region_11.12_spmd.clone, body=%wide.region_8.11_spmd.clone.sunk | while | flops 430987520 | bytes 32855764 | solution.py:135
  252.0 3.5 fusion.95
  255.5 2.9 fusion.97
  262.5 3.5 fusion.95
  266.1 2.9 fusion.97
  273.1 3.5 fusion.95
  276.7 2.9 fusion.97
  283.7 3.5 fusion.95
  294.3 3.5 fusion.95
  304.8 3.5 fusion.95
  315.4 3.5 fusion.95
  326.0 3.5 fusion.95
  337.6 5.0 convolution_convert_fusion
  342.7 77.5 %reduce-scatter.3.cloned.1.call-done = bf16[640,320]{0,1:T(8,128)(2,1)} async-done(((bf16[640,5120]{0,1:T(8,128)(2,1)}), bf16[640,320]{0,1:T(8,128)(2,1)}) %reduce-scatter.3.cloned.1.call-update) | async-done | bytes 409616 | tf_op jit(solution)/shard_map/reduce_scatter | solution.py:144
  422.2 29.1 %all-reduce = (f32[640]{0:T(1024)S(1)}, f32[640]{0:T(1024)S(1)}) all-reduce(f32[640]{0:T(1024)S(1)} %get-tuple-element.122, f32[640]{0:T(1024)S(1)} %get-tuple-element.121), channel_id=1, replica_groups=mesh['seq'=8,'hid'=16] {'hid'}, use_global_device_ids=true, to_apply=%region_16.17 | all-reduce | flops 1280 | bytes 10240 | tf_op jit(solution)/shard_map/psum | solution.py:23
  455.6 41.8 %all-gather.12.cloned.1.call-done = bf16[640,5120]{0,1:T(8,128)(2,1)} async-done(((bf16[640,320]{0,1:T(8,128)(2,1)}), bf16[640,5120]{0,1:T(8,128)(2,1)}) %all-gather.12.cloned.1.call-update) | async-done | bytes 6553616 | tf_op jit(solution)/shard_map/all_gather | solution.py:158
  497.4 7.6 %fusion.73 = f32[640,512]{1,0:T(8,128)S(1)} fusion(bf16[640,5120]{0,1:T(8,128)(2,1)} %all-gather.12.cloned.1.call-done, bf16[5120,512]{1,0:T(8,128)(2,1)} %param.24), kind=kOutput, calls=%fused_computation.112 | convolution fusion | flops 3355443200 | bytes 13107200 | tf_op jit(solution)/shard_map/dot_general | solution.py:157
  505.0 9.5 %convolution_convert_fusion.1 = bf16[640,5120]{0,1:T(8,128)(2,1)} fusion(bf16[512,5120]{1,0:T(8,128)(2,1)} %param.25, f32[640,512]{1,0:T(8,128)S(1)} %fusion.73), kind=kOutput, calls=%fused_computation.26 | convolution fusion | flops 3361669120 | bytes 13107200 | tf_op jit(solution)/shard_map/dot_general | solution.py:164
  514.5 80.6 %reduce-scatter.5.cloned.1.call-done = bf16[640,320]{0,1:T(8,128)(2,1)} async-done(((bf16[640,5120]{0,1:T(8,128)(2,1)}), bf16[640,320]{0,1:T(8,128)(2,1)}) %reduce-scatter.5.cloned.1.call-update) | async-done | bytes 409616 | tf_op jit(solution)/shard_map/reduce_scatter | solution.py:163
  (163 shorter events, 65.5 us)
Async XLA Ops:
  6.5 331.1 %copy-start = (bf16[256,5120]{1,0:T(8,128)(2,1)S(1)}, bf16[256,5120]{1,0:T(8,128)(2,1)}, u32[]{:S(2)}) copy-start(bf16[256,5120]{1,0:T(8,128)(2,1)} %param.23) | copy-start | bytes 7864324
  6.5 84.2 %all-gather.6.cloned.1.call-start = ((), (), s32[]{:S(2)}) async-start(), calls=%async_computation.2 | async-start | bytes 6963200 | tf_op jit(solution)/shard_map/all_gather | solution.py:74
  7.8 36.2 %copy-start.7 = (s32[640]{0:T(1024)S(1)}, s32[640]{0:T(1024)}, u32[]{:S(2)}) copy-start(s32[640]{0:T(1024)} %param.15) | copy-start | bytes 7684
  7.8 36.2 %copy-start.11 = (s32[8]{0:T(128)S(1)}, s32[8]{0:T(128)}, u32[]{:S(2)}) copy-start(s32[8]{0:T(128)} %param.16) | copy-start | bytes 100
  7.8 36.6 %copy-start.3 = (bf16[640,320]{0,1:T(8,128)(2,1)S(1)}, bf16[640,320]{0,1:T(8,128)(2,1)}, u32[]{:S(2)}) copy-start(bf16[640,320]{0,1:T(8,128)(2,1)} %param.14) | copy-start | bytes 1228804
  48.4 139.7 %all-gather.8.cloned.1.call-start = ((), (), s32[]{:S(2)}) async-start(), calls=%async_computation.3 | async-start | bytes 2949120 | tf_op jit(solution)/shard_map/all_gather | solution.py:122
  90.7 6.0 copy-start.2
  90.7 6.2 %copy-start.10 = (bf16[5120,256]{1,0:T(8,128)(2,1)S(1)}, bf16[5120,256]{1,0:T(8,128)(2,1)}, u32[]{:S(2)}) copy-start(bf16[5120,256]{1,0:T(8,128)(2,1)} %param.18) | copy-start | bytes 7864324
  97.0 33.7 %copy-start.8 = (f32[256]{0:T(256)S(1)}, f32[256]{0:T(256)}, u32[]{:S(2)}) copy-start(f32[256]{0:T(256)} %param.22) | copy-start | bytes 3076
  131.5 40.7 %copy-start.9 = (f32[256]{0:T(256)S(1)}, f32[256]{0:T(256)}, u32[]{:S(2)}) copy-start(f32[256]{0:T(256)} %param.21) | copy-start | bytes 3076
  131.5 115.1 %all-gather.10.cloned.1.call-start = ((), (), s32[]{:S(2)}) async-start(), calls=%async_computation.4 | async-start | bytes 2949120 | tf_op jit(solution)/shard_map/all_gather | solution.py:123
  137.9 282.4 %reduce-scatter.3.cloned.1.call-start = ((), (), s32[]{:S(2)}) async-start(), calls=%async_computation.5 | async-start | bytes 6963200 | tf_op jit(solution)/shard_map/reduce_scatter | solution.py:144
  255.5 4.2 copy-start.1
  255.5 4.2 copy-start.5
  266.1 4.2 copy-start.1
  266.1 4.2 copy-start.5
  276.6 4.2 copy-start.1
  276.7 4.2 copy-start.5
  282.5 0.8 copy-start.6
  287.2 4.2 copy-start.1
  287.2 4.2 copy-start.5
  297.8 4.2 copy-start.1
  297.8 4.2 copy-start.5
  308.4 4.2 copy-start.1
  308.4 4.2 copy-start.5
  319.0 4.2 copy-start.1
  319.0 4.2 copy-start.5
  329.5 4.2 copy-start.1
  329.6 4.2 copy-start.5
  342.7 77.6 %copy-start.4 = (bf16[640,320]{0,1:T(8,128)(2,1)S(1)}, bf16[640,320]{0,1:T(8,128)(2,1)}, u32[]{:S(2)}) copy-start(bf16[640,320]{0,1:T(8,128)(2,1)} %param.14) | copy-start | bytes 1228804
  342.7 154.7 %all-gather.12.cloned.1.call-start = ((), (), s32[]{:S(2)}) async-start(), calls=%async_computation.6 | async-start | bytes 6963200 | tf_op jit(solution)/shard_map/all_gather | solution.py:158
  455.3 139.8 %reduce-scatter.5.cloned.1.call-start = ((), (), s32[]{:S(2)}) async-start(), calls=%async_computation.7 | async-start | bytes 6963200 | tf_op jit(solution)/shard_map/reduce_scatter | solution.py:163
  (7 other events, 5.9 us)
Sparse Core Ops, SparseCore 0:
  48.6 42.1 all-gather.5
  131.6 56.4 all-gather.7
  190.5 56.1 all-gather.9
  342.8 77.3 reduce-scatter.2
  455.4 41.9 all-gather.11
  514.6 80.4 reduce-scatter.4
where the time goes:
time: 606 us; the launch traced here: 605 us
  waiting for transfers between devices  307 us (51%)
  blocking collectives  126 us (21%)
  matrix products  91.5 us (15%)
  local copies, waits for them, and re-layouts  36 us (6%)
  other arithmetic  29.8 us (5%)
  between operations  13.7 us (2%)
    reduce_scatter x1, waiting for transfers between devices, shards(): lax.psum_scatter(jnp.dot(hidden, w_down, preferred_element_type=jnp.float...  80.6 us
    reduce_scatter x1, waiting for transfers between devices, shards(): lax.psum_scatter(out_terms.astype(jnp.bfloat16), 'hid', scatter_dimension...  77.5 us
    psum x2, blocking collectives, shared_moments(): lax.psum((jnp.sum(values, axis=1), jnp.sum(values * values, axis=1)), 'hid')  61.2 us
    all_gather x1, waiting for transfers between devices, shards(): value_piece = lax.all_gather(value_rows, 'seq', axis=0, tiled=True)  49.9 us
    all_gather x1, waiting for transfers between devices, shards(): pieces = lax.all_gather(normed, 'hid', axis=1, tiled=True)  42.2 us
    all_gather x1, waiting for transfers between devices, shards(): lax.all_gather(normed_ffn, 'hid', axis=1, tiled=True)  41.8 us
    all_gather x1, blocking collectives, shards(): mark_piece = lax.all_gather(clip_marks, 'seq', axis=0, tiled=True)  34.2 us
    psum x1, blocking collectives, shards(): lax.psum((jnp.sum(queries * queries, axis=1), jnp.sum(key_proj * key_proj...  30.5 us
  transfers between devices with their start and end apart: 6, of which 6 were waited for; matrix products, arithmetic and copies ran while one was open for 3% of the time, Pallas kernels for 0%

commit v1 on v0

--- a/solution.py
+++ b/solution.py
@@ -119,7 +119,9 @@
         jnp.zeros((heads_here, tok_rows), jnp.float32),
         jnp.zeros((heads_here, tok_rows, HEAD_DIM), jnp.float32),
     )
-    key_piece = lax.all_gather(k_normed, "seq", axis=0, tiled=True)
+    key_piece = jnp.concatenate(
+        lax.all_to_all(jnp.stack([k_normed] * lax.axis_size("seq")), "seq", 0, 0), axis=0
+    )
     value_piece = lax.all_gather(value_rows, "seq", axis=0, tiled=True)
     mark_piece = lax.all_gather(clip_marks, "seq", axis=0, tiled=True)
     tile_count = key_piece.shape[0] // tok_rows

time: 606 us -> 565 us (0.932)
  waiting for transfers between devices: 307 us -> 240 us
  blocking collectives: 126 us -> 150 us
  local copies, waits for them, and re-layouts: 36 us -> 29.1 us
  starting transfers between devices: 0.43 us -> 7.29 us
    all_gather x1, waiting for transfers between devices: 49.9 us -> 0.02 us  [shards(): value_piece = lax.all_gather(value_rows, 'seq', axis=0, tiled=True)]
    all_gather x1, blocking collectives: 34.2 us -> 57.5 us  [shards(): mark_piece = lax.all_gather(clip_marks, 'seq', axis=0, tiled=True)]
    all_gather x1 -> x0, waiting for transfers between devices: 14.6 us -> none  [shards(): key_piece = lax.all_gather(k_normed, 'seq', axis=0, tiled=True)]
    unnamed x23 -> x19, local copies, waits for them, and re-layouts: 9.06 us -> 0.27 us
    all_to_all x0 -> x1, starting transfers between devices: none -> 6.91 us  [shards(): lax.all_to_all(jnp.stack([k_normed] * lax.axis_size('seq')), 'seq', 0, 0)]
  transfers between devices with their start and end apart: 6 -> 6, of which waited for: 6 -> 4; matrix products, arithmetic and copies ran while one was open for 3% -> 4% of each run, Pallas kernels for 0% -> 0%
where the time goes in v1:
time: 565 us; the launch traced here: 564 us
  waiting for transfers between devices  240 us (42%)
  blocking collectives  150 us (27%)
  matrix products  94.9 us (17%)
  local copies, waits for them, and re-layouts  29.1 us (5%)
  other arithmetic  29.1 us (5%)
  between operations  13.4 us (2%)
  starting transfers between devices  7.29 us (1%)
    reduce_scatter x1, waiting for transfers between devices, shards(): lax.psum_scatter(jnp.dot(hidden, w_down, preferred_element_type=jnp.float...  80.6 us
    reduce_scatter x1, waiting for transfers between devices, shards(): lax.psum_scatter(out_terms.astype(jnp.bfloat16), 'hid', scatter_dimension...  75.7 us
    psum x2, blocking collectives, shared_moments(): lax.psum((jnp.sum(values, axis=1), jnp.sum(values * values, axis=1)), 'hid')  61.2 us
    all_gather x1, blocking collectives, shards(): mark_piece = lax.all_gather(clip_marks, 'seq', axis=0, tiled=True)  57.5 us
    all_gather x1, waiting for transfers between devices, shards(): pieces = lax.all_gather(normed, 'hid', axis=1, tiled=True)  42.2 us
    all_gather x1, waiting for transfers between devices, shards(): lax.all_gather(normed_ffn, 'hid', axis=1, tiled=True)  41.8 us
    psum x1, blocking collectives, shards(): lax.psum((jnp.sum(queries * queries, axis=1), jnp.sum(key_proj * key_proj...  30.9 us
    dot_general x8, matrix products, tile_update(): jnp.einsum('qhd,khd->hqk', q_heads, key_tile, preferred_element_type=jnp....  28.9 us
  transfers between devices with their start and end apart: 6, of which 4 were waited for; matrix products, arithmetic and copies ran while one was open for 4% of the time, Pallas kernels for 0%

profile of v1, /device:TPU:0, one launch (start us, length us, event | category | flops | bytes accessed | tf_op | source)
XLA Modules:
  0.0 564.2 jit_solution(15628216427623157672)
XLA Ops:
  7.9 4.2 fusion.72
  12.1 32.1 %all-reduce.2 = (f32[640]{0:T(1024)S(1)}, f32[640]{0:T(1024)S(1)}) all-reduce(f32[640]{0:T(1024)S(1)} %get-tuple-element.124, f32[640]{0:T(1024)S(1)} %get-tuple-element.123), channel_id=1, replica_groups=mesh['seq'=8,'hid'=16] {'hid'}, use_global_device_ids=true, to_apply=%region_3.0 | all-reduce | flops 1280 | bytes 10240 | tf_op jit(solution)/shard_map/psum | solution.py:23
  48.7 42.2 %all-gather.5.cloned.1.call-done = bf16[640,5120]{0,1:T(8,128)(2,1)} async-done(((bf16[640,320]{0,1:T(8,128)(2,1)}), bf16[640,5120]{0,1:T(8,128)(2,1)}) %all-gather.5.cloned.1.call-update) | async-done | bytes 6553616 | tf_op jit(solution)/shard_map/all_gather | solution.py:74
  90.9 6.2 %convolution_convert_fusion.2 = bf16[640,256]{1,0:T(8,128)(2,1)} fusion(bf16[640,5120]{0,1:T(8,128)(2,1)} %all-gather.5.cloned.1.call-done, bf16[5120,256]{1,0:T(8,128)(2,1)} %param.20), kind=kOutput, calls=%fused_computation.56 | convolution fusion | flops 1677885440 | bytes 9502720 | tf_op jit(solution)/shard_map/dot_general | solution.py:77
  97.2 6.0 %multiply_reduce_fusion.1 = (f32[640]{0:T(1024)S(1)}, f32[640,256]{0,1:T(8,128)S(1)}) fusion(bf16[640,5120]{0,1:T(8,128)(2,1)} %all-gather.5.cloned.1.call-done, bf16[5120,256]{1,0:T(8,128)(2,1)} %param.19), kind=kOutput, calls=%fused_computation.70 | convolution fusion | flops 1678048640 | bytes 9832960 | tf_op jit(solution)/shard_map/dot_general | solution.py:77
  103.2 5.9 %multiply_reduce_fusion = (f32[640]{0:T(1024)S(1)}, f32[640,256]{0,1:T(8,128)}) fusion(bf16[640,5120]{0,1:T(8,128)(2,1)} %all-gather.5.cloned.1.call-done, bf16[5120,256]{1,0:T(8,128)(2,1)S(1)} %copy-done.9), kind=kOutput, calls=%fused_computation.68 | convolution fusion | flops 1678048640 | bytes 9832960 | tf_op jit(solution)/shard_map/dot_general | solution.py:77
  109.2 30.9 %all-reduce.1 = (f32[640]{0:T(1024)S(1)}, f32[640]{0:T(1024)S(1)}) all-reduce(f32[640]{0:T(1024)S(1)} %get-tuple-element.163, f32[640]{0:T(1024)S(1)} %get-tuple-element.165), channel_id=1, replica_groups=mesh['seq'=8,'hid'=16] {'hid'}, use_global_device_ids=true, to_apply=%region_5.0 | all-reduce | flops 1280 | bytes 10240 | tf_op jit(solution)/shard_map/psum | solution.py:82
  141.9 6.9 %all-to-all-start = ((bf16[8,640,256]{1,2,0:T(8,128)(2,1)}), bf16[8,640,256]{1,2,0:T(8,128)(2,1)}, u32[]{:S(2)}, u32[]{:S(2)}) async-start(bf16[8,640,256]{1,2,0:T(8,128)(2,1)} %stack.2), calls=%async_computation | async-start | bytes 5242880 | tf_op jit(solution)/shard_map/all_to_all | solution.py:123
  148.9 57.5 %all-gather = bf16[8,1,640]{2,1,0:T(2,128)(2,1)S(1)} all-gather(bf16[1,1,640]{2,1,0:T(2,128)(2,1)S(1)} %reshape.73), channel_id=1, replica_groups=mesh['seq'=8,'hid'=16] {'seq'}, dimensions={0}, use_global_device_ids=true | all-gather | bytes 11520 | tf_op jit(solution)/shard_map/all_gather | solution.py:126
  207.9 4.9 reshape.71
  212.9 85.2 %while.15 = (s32[]{:T(128)}, f32[2,640]{1,0:T(2,128)S(1)}, f32[2,640]{1,0:T(2,128)S(1)}, f32[2,640,128]{2,1,0:T(8,128)}, bf16[640]{0:T(1024)(128)(2,1)S(1)}, /*i...) while((s32[]{:T(128)}, f32[2,640]{1,0:T(2,128)S(1)}, ...), condition=%wide.region_11.12_spmd.clone, body=%wide.region_8.11_spmd.clone.sunk | while | flops 430987520 | bytes 32855764 | solution.py:137
  213.2 3.6 fusion.95
  216.8 2.9 fusion.97
  223.9 3.6 fusion.95
  227.5 2.9 fusion.97
  234.5 3.6 fusion.95
  245.2 3.6 fusion.95
  248.8 2.9 fusion.97
  255.8 3.6 fusion.95
  259.4 2.9 fusion.97
  266.5 3.6 fusion.95
  270.1 2.9 fusion.97
  277.1 3.6 fusion.95
  287.8 3.6 fusion.95
  291.4 2.9 fusion.97
  299.5 5.0 convolution_convert_fusion
  304.5 75.7 %reduce-scatter.3.cloned.1.call-done = bf16[640,320]{0,1:T(8,128)(2,1)} async-done(((bf16[640,5120]{0,1:T(8,128)(2,1)}), bf16[640,320]{0,1:T(8,128)(2,1)}) %reduce-scatter.3.cloned.1.call-update) | async-done | bytes 409616 | tf_op jit(solution)/shard_map/reduce_scatter | solution.py:146
  382.1 29.1 %all-reduce = (f32[640]{0:T(1024)S(1)}, f32[640]{0:T(1024)S(1)}) all-reduce(f32[640]{0:T(1024)S(1)} %get-tuple-element.122, f32[640]{0:T(1024)S(1)} %get-tuple-element.121), channel_id=1, replica_groups=mesh['seq'=8,'hid'=16] {'hid'}, use_global_device_ids=true, to_apply=%region_16.17 | all-reduce | flops 1280 | bytes 10240 | tf_op jit(solution)/shard_map/psum | solution.py:23
  415.5 41.8 %all-gather.9.cloned.1.call-done = bf16[640,5120]{0,1:T(8,128)(2,1)} async-done(((bf16[640,320]{0,1:T(8,128)(2,1)}), bf16[640,5120]{0,1:T(8,128)(2,1)}) %all-gather.9.cloned.1.call-update) | async-done | bytes 6553616 | tf_op jit(solution)/shard_map/all_gather | solution.py:160
  457.3 7.6 %fusion.73 = f32[640,512]{1,0:T(8,128)S(1)} fusion(bf16[640,5120]{0,1:T(8,128)(2,1)} %all-gather.9.cloned.1.call-done, bf16[5120,512]{1,0:T(8,128)(2,1)} %param.24), kind=kOutput, calls=%fused_computation.112 | convolution fusion | flops 3355443200 | bytes 13107200 | tf_op jit(solution)/shard_map/dot_general | solution.py:159
  464.9 9.6 %convolution_convert_fusion.1 = bf16[640,5120]{0,1:T(8,128)(2,1)} fusion(bf16[512,5120]{1,0:T(8,128)(2,1)} %param.25, f32[640,512]{1,0:T(8,128)S(1)} %fusion.73), kind=kOutput, calls=%fused_computation.26 | convolution fusion | flops 3361669120 | bytes 13107200 | tf_op jit(solution)/shard_map/dot_general | solution.py:166
  474.5 80.6 %reduce-scatter.5.cloned.1.call-done = bf16[640,320]{0,1:T(8,128)(2,1)} async-done(((bf16[640,5120]{0,1:T(8,128)(2,1)}), bf16[640,320]{0,1:T(8,128)(2,1)}) %reduce-scatter.5.cloned.1.call-update) | async-done | bytes 409616 | tf_op jit(solution)/shard_map/reduce_scatter | solution.py:165
  (158 shorter events, 57.4 us)
Async XLA Ops:
  6.5 292.9 %copy-start = (bf16[256,5120]{1,0:T(8,128)(2,1)S(1)}, bf16[256,5120]{1,0:T(8,128)(2,1)}, u32[]{:S(2)}) copy-start(bf16[256,5120]{1,0:T(8,128)(2,1)} %param.23) | copy-start | bytes 7864324
  6.5 84.4 %all-gather.5.cloned.1.call-start = ((), (), s32[]{:S(2)}) async-start(), calls=%async_computation.3 | async-start | bytes 6963200 | tf_op jit(solution)/shard_map/all_gather | solution.py:74
  7.8 36.4 %copy-start.6 = (s32[640]{0:T(1024)S(1)}, s32[640]{0:T(1024)}, u32[]{:S(2)}) copy-start(s32[640]{0:T(1024)} %param.15) | copy-start | bytes 7684
  7.8 36.4 %copy-start.10 = (s32[8]{0:T(128)S(1)}, s32[8]{0:T(128)}, u32[]{:S(2)}) copy-start(s32[8]{0:T(128)} %param.16) | copy-start | bytes 100
  7.8 36.8 %copy-start.2 = (bf16[640,320]{0,1:T(8,128)(2,1)S(1)}, bf16[640,320]{0,1:T(8,128)(2,1)}, u32[]{:S(2)}) copy-start(bf16[640,320]{0,1:T(8,128)(2,1)} %param.14) | copy-start | bytes 1228804
  48.6 159.3 %all-gather.7.cloned.1.call-start = ((), (), s32[]{:S(2)}) async-start(), calls=%async_computation.4 | async-start | bytes 2949120 | tf_op jit(solution)/shard_map/all_gather | solution.py:125
  97.2 6.0 %copy-start.9 = (bf16[5120,256]{1,0:T(8,128)(2,1)S(1)}, bf16[5120,256]{1,0:T(8,128)(2,1)}, u32[]{:S(2)}) copy-start(bf16[5120,256]{1,0:T(8,128)(2,1)} %param.18) | copy-start | bytes 7864324
  103.2 36.9 %copy-start.7 = (f32[256]{0:T(256)S(1)}, f32[256]{0:T(256)}, u32[]{:S(2)}) copy-start(f32[256]{0:T(256)} %param.22) | copy-start | bytes 3076
  141.9 64.6 %copy-start.8 = (f32[256]{0:T(256)S(1)}, f32[256]{0:T(256)}, u32[]{:S(2)}) copy-start(f32[256]{0:T(256)} %param.21) | copy-start | bytes 3076
  141.9 70.9 %all-to-all-start = ((bf16[8,640,256]{1,2,0:T(8,128)(2,1)}), bf16[8,640,256]{1,2,0:T(8,128)(2,1)}, u32[]{:S(2)}, u32[]{:S(2)}) async-start(bf16[8,640,256]{1,2,0:T(8,128)(2,1)} %stack.2), calls=%async_computation | async-start | bytes 5242880 | tf_op jit(solution)/shard_map/all_to_all | solution.py:123
  148.8 231.4 %reduce-scatter.3.cloned.1.call-start = ((), (), s32[]{:S(2)}) async-start(), calls=%async_computation.5 | async-start | bytes 6963200 | tf_op jit(solution)/shard_map/reduce_scatter | solution.py:146
  216.8 4.2 copy-start.1
  216.8 4.2 copy-start.4
  222.7 0.8 copy-start.5
  227.5 4.2 copy-start.1
  227.5 4.2 copy-start.4
  233.3 0.8 copy-start.5
  238.1 4.2 copy-start.1
  238.1 4.2 copy-start.4
  248.8 4.2 copy-start.1
  248.8 4.2 copy-start.4
  259.4 4.2 copy-start.1
  259.4 4.2 copy-start.4
  270.1 4.2 copy-start.1
  270.1 4.2 copy-start.4
  280.7 4.2 copy-start.1
  280.7 4.2 copy-start.4
  291.4 4.2 copy-start.1
  291.4 4.2 copy-start.4
  304.5 75.7 %copy-start.3 = (bf16[640,320]{0,1:T(8,128)(2,1)S(1)}, bf16[640,320]{0,1:T(8,128)(2,1)}, u32[]{:S(2)}) copy-start(bf16[640,320]{0,1:T(8,128)(2,1)} %param.14) | copy-start | bytes 1228804
  304.5 152.8 %all-gather.9.cloned.1.call-start = ((), (), s32[]{:S(2)}) async-start(), calls=%async_computation.6 | async-start | bytes 6963200 | tf_op jit(solution)/shard_map/all_gather | solution.py:160
  415.3 139.9 %reduce-scatter.5.cloned.1.call-start = ((), (), s32[]{:S(2)}) async-start(), calls=%async_computation.7 | async-start | bytes 6963200 | tf_op jit(solution)/shard_map/reduce_scatter | solution.py:165
  (6 other events, 5.1 us)
Sparse Core Ops, SparseCore 0:
  48.7 42.1 all-gather.4
  97.3 72.9 all-gather.6
  304.6 75.5 reduce-scatter.2
  415.4 41.9 all-gather.8
  474.6 80.4 reduce-scatter.4
